TPU v7x, 32 devices: a whole 2x2x4 slice. The times are simulated.
32 devices in a mesh: groups: 2 (over y), replica: 4 (over z), tensor: 4 (over x, core).
Axes of the slice: x: 2, y: 2, z: 4, core: 2. Of those that a mesh axis runs over, the one named last changes fastest.
Arguments:
- queries: bfloat16 [144, 8192], P(('groups', 'replica'), 'tensor'), parts along dimension 0, may hold values from -64 to 64
- past_cache: bfloat16 [2, 144, 128, 1024], P(None, ('groups', 'replica'), None, 'tensor'), parts along dimension 1, may hold values from -6 to 6
- lengths: int32 [144], P(('groups', 'replica')), parts along dimension 0, may hold values from 2 to 128, as said below
- live_counts: int32 [8], P(('groups', 'replica')), parts along dimension 0, may hold values from 1 to 16, as said below
- adapter_index: int32 [144], P(('groups', 'replica')), parts along dimension 0, may hold values from 0 to 15, as said below
- adapter_down: bfloat16 [16, 16, 8192], P('replica', None, 'tensor'), may hold values from -0.0625 to 0.0625
- adapter_up: bfloat16 [16, 16, 8192], P('replica', None, 'tensor'), may hold values from -6 to 6
Outputs:
- attention: bfloat16 [144, 8192], P(('groups', 'replica'), 'tensor'), parts along dimension 0
- adapted: bfloat16 [144, 8192], P(('groups', 'replica'), 'tensor'), parts along dimension 0
There are 2 independent parts, one for each index of `groups`. A program takes and returns all parts, laid end to end along the dimension named above; an argument that names none is the same for every part. Nothing has to cross between parts.
Inputs may be any that keep to these rules, and one draw needn't show every extreme that they name: `adapter_index`: over the first 16 slots of all replicas, exactly 4 distinct adapters appear, homed on 4 distinct replicas. Each of the last 2 slots of a replica names an adapter outside that set; the homes (adapter a lives on replica a // 4) of one replica's last 2 slots are distinct, and some replica is the home of one such slot of every replica. `lengths`: some request has exactly 128. `live_counts`: some replica has exactly 16.
All inputs are finite; a program needn't handle non-finite values.
Results may differ from a plain program's by a relative error of at most 0.008.
Values may be sent and summed in bfloat16 or wider, within the bound.
A program may use at most 64 MiB of HBM per device.

v0:
```python
import math
import jax
import jax.numpy as jnp
from jax import lax
from jax.sharding import PartitionSpec as P

HEAD_DIM = 128
STAY = 16
SCALING = 2.0


def broadcast(block, axis, owner):
    block = jnp.where(lax.axis_index(axis) == owner, block, jnp.zeros_like(block))
    return lax.psum(block, axis)


def attend(queries, keys, values, visible):
    count = queries.shape[0]
    key_width = keys.shape[-1]
    key_heads = key_width // HEAD_DIM
    group_size = queries.shape[1] // key_width
    context = keys.shape[1]
    query_rows = queries.reshape(count, key_heads, group_size, HEAD_DIM)
    key_rows = keys.reshape(count, context, key_heads, HEAD_DIM)
    value_rows = values.reshape(count, context, key_heads, HEAD_DIM)
    scores = jnp.einsum(
        "nhgd,nlhd->nhgl", query_rows, key_rows, preferred_element_type=jnp.float32
    ) / math.sqrt(HEAD_DIM)
    scores = jnp.where(visible[:, None, None, :], scores, -jnp.inf)
    peak = jnp.max(scores, axis=-1, keepdims=True)
    raised = jnp.exp(scores - peak)
    weights = (raised / jnp.sum(raised, axis=-1, keepdims=True)).astype(jnp.bfloat16)
    mixed = jnp.einsum("nhgl,nlhd->nhgd", weights, value_rows, preferred_element_type=jnp.float32)
    return mixed.reshape(count, key_heads * group_size * HEAD_DIM)


def widen_rows(rank_rows, up_rows):
    widened = jnp.einsum("nr,nrc->nc", rank_rows, up_rows.astype(jnp.float32))
    return (SCALING * widened).astype(jnp.bfloat16)


def on_device(queries, past_cache, lengths, live_counts, adapter_index, adapter_down, adapter_up):
    slots = queries.shape[0]
    moving = slots - STAY
    replicas = lax.axis_size("replica")
    hot_total = min(8, replicas)
    local_count = adapter_down.shape[0]
    total_adapters = local_count * replicas
    context = past_cache.shape[2]
    position = jnp.arange(context, dtype=jnp.int32)
    slot_index = jnp.arange(slots, dtype=jnp.int32)
    alive = (slot_index >= STAY) | (slot_index < live_counts[0])
    visible = position[None, :] < lengths[:, None]
    stay_index = adapter_index[:STAY]
    catalog = jnp.arange(total_adapters, dtype=jnp.int32)
    usage = jnp.sum((stay_index[:, None] == catalog[None, :]).astype(jnp.int32), axis=0)
    usage = lax.psum(usage, "replica")
    ranking = jnp.where(usage > 0, total_adapters - catalog, 0)
    hot_index = total_adapters - lax.top_k(ranking, hot_total)[0]
    down_list = []
    up_list = []
    for hot_slot in range(hot_total):
        holder = hot_index[hot_slot] // local_count
        within = hot_index[hot_slot] % local_count
        local_pair = (
            lax.dynamic_index_in_dim(adapter_down, within, 0, False),
            lax.dynamic_index_in_dim(adapter_up, within, 0, False),
        )
        fetched = (
            broadcast(local_pair[0], "replica", holder),
            broadcast(local_pair[1], "replica", holder),
        )
        down_list.append(fetched[0])
        up_list.append(fetched[1])
    hot_down = jnp.stack(down_list)
    hot_up = jnp.stack(up_list)
    hot_pick = (stay_index[:, None] == hot_index[None, :]).astype(jnp.bfloat16)
    stay_down = jnp.einsum("nh,hrc->nrc", hot_pick, hot_down)
    stay_up = jnp.einsum("nh,hrc->nrc", hot_pick, hot_up)
    stay_attention = attend(
        queries[:STAY], past_cache[0, :STAY], past_cache[1, :STAY], visible[:STAY]
    )
    stay_attention = jnp.where(alive[:STAY, None], stay_attention, 0.0).astype(jnp.bfloat16)
    stay_partial = jnp.einsum(
        "nc,nrc->nr", stay_attention, stay_down, preferred_element_type=jnp.float32
    )
    moved_index = adapter_index[STAY:]
    homes = moved_index // local_count
    replica_ids = jnp.arange(replicas, dtype=jnp.int32)
    matched = homes[None, :] == replica_ids[:, None]
    occupied = jnp.any(matched, axis=1)
    source_slot = jnp.sum(
        jnp.where(matched, jnp.arange(moving, dtype=jnp.int32)[None, :], 0), axis=1
    )
    wanted = jnp.where(occupied, jnp.take(moved_index, source_slot) % local_count, -1)
    local_catalog = jnp.arange(local_count, dtype=jnp.int32)
    chooser = (
        lax.all_to_all(wanted[:, None], "replica", split_axis=0, concat_axis=0, tiled=True)[
            :, :, None
        ]
        == local_catalog[None, None, :]
    ).astype(jnp.bfloat16)
    send_down = jnp.einsum("sna,arc->snrc", chooser, adapter_down)
    send_up = jnp.einsum("sna,arc->snrc", chooser, adapter_up)
    got_down = lax.all_to_all(send_down, "replica", split_axis=0, concat_axis=0, tiled=True)
    got_up = lax.all_to_all(send_up, "replica", split_axis=0, concat_axis=0, tiled=True)
    moved_down = jnp.take(got_down[:, 0], homes, axis=0)
    moved_up = jnp.take(got_up[:, 0], homes, axis=0)
    moved_attention = attend(
        queries[STAY:], past_cache[0, STAY:], past_cache[1, STAY:], visible[STAY:]
    ).astype(jnp.bfloat16)
    moved_partial = jnp.einsum(
        "nc,nrc->nr", moved_attention, moved_down, preferred_element_type=jnp.float32
    )
    rank_rows = lax.psum(jnp.concatenate([stay_partial, moved_partial], axis=0), "tensor")
    stay_adapted = widen_rows(rank_rows[:STAY], stay_up)
    moved_adapted = widen_rows(rank_rows[STAY:], moved_up)
    attention = jnp.concatenate([stay_attention, moved_attention], axis=0)
    adapted = jnp.concatenate([stay_adapted, moved_adapted], axis=0)
    return (attention, adapted)


def solution(mesh):
    in_specs = (
        P(("groups", "replica"), "tensor"),
        P(None, ("groups", "replica"), None, "tensor"),
        P(("groups", "replica")),
        P(("groups", "replica")),
        P(("groups", "replica")),
        P("replica", None, "tensor"),
        P("replica", None, "tensor"),
    )
    out_specs = (P(("groups", "replica"), "tensor"), P(("groups", "replica"), "tensor"))
    return jax.shard_map(
        on_device, mesh=mesh, in_specs=in_specs, out_specs=out_specs, check_vma=False
    )
```

profile of v0, /device:TPU:0, one launch (start us, length us, event | category | flops | bytes accessed | tf_op | source)
XLA Modules:
  0.0 125.1 jit_solution(2885234638877340328)
XLA Ops:
  7.2 0.7 compare_and_fusion
  7.9 0.7 slice.70
  8.6 0.1 fusion.54
  8.7 0.1 select_reduce_fusion
  8.8 0.6 gather_fusion
  9.5 0.7 copy.78
  10.1 6.3 %all-to-all-start = ((s32[4,1,1]{2,1,0:T(1,128)}), s32[4,1,1]{2,1,0:T(1,128)S(1)}, u32[]{:S(2)}, u32[]{:S(2)}) async-start(s32[4,1,1]{2,1,0:T(1,128)} %copy.78), calls=%async_computation | async-start | bytes 4096 | tf_op jit(solution)/shard_map/all_to_all | solution.py:98
  16.5 0.0 all-reduce.3.cloned.1.call-start
  16.5 0.7 convert_reduce_fusion
  17.2 8.8 %psum.70 = s32[16]{0:T(128)S(1)} all-reduce(s32[16]{0:T(128)S(1)} %convert_reduce_fusion), channel_id=1, replica_groups=mesh['groups'=2,'replica'=4,'tensor'=4] {'replica'}, use_global_device_ids=true, to_apply=%region_5.6 | all-reduce | flops 16 | bytes 128 | tf_op jit(solution)/shard_map/psum | solution.py:57
  26.1 1.2 top_k.9
  27.3 0.7 fusion.67
  38.2 1.2 copy.73
  39.4 1.2 copy.81
  40.6 1.4 %broadcast_select_fusion.7 = (bf16[1,16,2048]{2,0,1:T(2,128)(2,1)}, bf16[1,16,2048]{2,0,1:T(2,128)(2,1)}, bf16[1,16,2048]{2,0,1:T(2,128)(2,1)}, bf16[1,16,2048]{2,0,1:T(2,128)(2,1)}) fusion(pred[]{:T(512)S(6)} %eq.87, bf16[4,16,2048]{2,0,1:T(4,128)(2,1)S(1)} %copy.73, s32[]{:T(128)S(6)} %select_n.215, s32[]{:T(128)S(6)} %select_n.233, pred[]{:T(512)S(6)} %eq.90, ...), kind=kLoop, calls=%fused_computation.43 | loop fusion | flops 131072 | bytes 524308 | tf_op jit(solution)/shard_map/jit(_where)/select_n | solution.py:13
  42.0 1.5 %broadcast_select_fusion.6 = (bf16[1,16,2048]{2,0,1:T(2,128)(2,1)}, bf16[1,16,2048]{2,0,1:T(2,128)(2,1)}, bf16[1,16,2048]{2,0,1:T(2,128)(2,1)}, bf16[1,16,2048]{2,0,1:T(2,128)(2,1)}) fusion(pred[]{:T(512)S(6)} %eq.87, bf16[4,16,2048]{2,0,1:T(4,128)(2,1)S(1)} %copy.81, s32[]{:T(128)S(6)} %select_n.215, s32[]{:T(128)S(6)} %select_n.233, pred[]{:T(512)S(6)} %eq.90, ...), kind=kLoop, calls=%fused_computation.42 | loop fusion | flops 131072 | bytes 524308 | tf_op jit(solution)/shard_map/jit(_where)/select_n | solution.py:13
  43.5 0.0 all-reduce.3.cloned.1.call-update
  43.5 0.0 copy-start
  43.5 0.0 copy-start.1
  43.5 1.0 fusion.66
  44.6 1.7 %fusion.65 = (bf16[1,16,128,256]{3,2,1,0:T(8,128)(2,1)S(1)}, bf16[1,16,128,256]{3,2,1,0:T(8,128)(2,1)S(1)}) fusion(bf16[2,18,128,256]{3,2,1,0:T(8,128)(2,1)} %param.10), kind=kLoop, calls=%fused_computation.114 | loop fusion | bytes 4194304 | tf_op jit(solution)/shard_map/slice | solution.py:81
  46.3 0.0 copy-done
  46.3 0.0 copy-done.1
  46.3 0.1 iota_compare_fusion
  46.4 0.1 copy.105
  46.5 0.1 copy.104
  46.6 0.1 fusion.7
  46.8 0.2 fusion.68
  47.0 0.2 convolution_convert_fusion
  47.2 1.3 %copy.103 = bf16[1,16,128,256]{2,3,1,0:T(8,128)(2,1)} copy(bf16[1,16,128,256]{3,2,1,0:T(8,128)(2,1)S(1)} %get-tuple-element.17) | data formatting | bytes 2097152
  48.6 0.7 copy.102
  49.2 0.4 fusion.4
  49.6 0.2 fusion.69
  50.5 1.9 %fusion.37 = bf16[16,2,8,128]{3,2,1,0:T(8,128)(2,1)S(1)} fusion(bf16[16,128,2,128]{1,3,2,0:T(8,128)(2,1)} %bitcast.99, f32[16,2,8]{2,1,0:T(2,128)S(1)} %fusion.69, f32[16,2,8,128]{3,2,1,0:T(8,128)S(1)} %fusion.4), kind=kOutput, calls=%fused_computation.58 | convolution fusion | flops 8487295 | bytes 1246208 | tf_op jit(solution)/shard_map/nhgl,nlhd->nhgd/dot_general | solution.py:33
  52.4 0.0 copy-start.6
  52.4 0.1 fusion.28
  52.5 0.0 all-to-all-done
  52.5 0.2 reduce
  52.7 0.4 convolution_bitcast_fusion.1
  53.1 0.8 copy.80
  53.9 3.4 %all-to-all-start.1 = ((bf16[4,1,16,2048]{3,2,1,0:T(8,128)(2,1)}), bf16[4,1,16,2048]{3,2,1,0:T(8,128)(2,1)S(1)}, u32[]{:S(2)}, u32[]{:S(2)}) async-start(bf16[4,1,16,2048]{3,2,1,0:T(8,128)(2,1)} %copy.80), calls=%async_computation.1 | async-start | bytes 524288 | tf_op jit(solution)/shard_map/all_to_all | solution.py:105
  57.3 0.4 convolution_bitcast_fusion
  57.7 0.8 copy.86
  58.6 14.4 %all-to-all-done.1 = bf16[4,1,16,2048]{3,2,1,0:T(8,128)(2,1)S(1)} async-done(((bf16[4,1,16,2048]{3,2,1,0:T(8,128)(2,1)}), bf16[4,1,16,2048]{3,2,1,0:T(8,128)(2,1)S(1)}, u32[]{:S(2)}, u32[]{:S(2)}) %all-to-all-start.1) | async-done | bytes 262176 | tf_op jit(solution)/shard_map/all_to_all | solution.py:105
  72.9 3.4 %all-to-all-start.2 = ((bf16[4,1,16,2048]{3,2,1,0:T(8,128)(2,1)}), bf16[4,1,16,2048]{3,2,1,0:T(8,128)(2,1)S(1)}, u32[]{:S(2)}, u32[]{:S(2)}) async-start(bf16[4,1,16,2048]{3,2,1,0:T(8,128)(2,1)} %copy.86), calls=%async_computation.2 | async-start | bytes 524288 | tf_op jit(solution)/shard_map/all_to_all | solution.py:106
  76.4 0.1 fusion.84
  76.4 0.6 gather_fusion.1
  77.0 6.2 %all-to-all-done.2 = bf16[4,1,16,2048]{3,2,1,0:T(8,128)(2,1)S(1)} async-done(((bf16[4,1,16,2048]{3,2,1,0:T(8,128)(2,1)}), bf16[4,1,16,2048]{3,2,1,0:T(8,128)(2,1)S(1)}, u32[]{:S(2)}, u32[]{:S(2)}) %all-to-all-start.2) | async-done | bytes 262176 | tf_op jit(solution)/shard_map/all_to_all | solution.py:106
  83.1 0.6 gather_fusion.2
  83.7 0.2 fusion.33
  83.9 17.2 %all-reduce.3.cloned.1.call-done = (bf16[1,16,2048]{2,0,1:T(2,128)(2,1)}, bf16[1,16,2048]{2,0,1:T(2,128)(2,1)}, bf16[1,16,2048]{2,0,1:T(2,128)(2,1)}, bf16[1,16,...) async-done(((bf16[1,16,2048]{2,0,1:T(2,128)(2,1)}, ...) | async-done | bytes 524304 | tf_op jit(solution)/shard_map/psum | solution.py:14
  101.1 0.0 copy-start.2
  101.1 0.0 copy-done.6
  101.2 2.1 %fusion.12 = bf16[16,16,2048]{2,0,1:T(8,128)(2,1)S(1)} fusion(bf16[1,16,2048]{2,0,1:T(2,128)(2,1)} %get-tuple-element.6, bf16[1,16,2048]{2,0,1:T(2,128)(2,1)} %get-tuple-element.7, bf16[1,16,2048]{2,0,1:T(2,128)(2,1)} %get-tuple-element.8, bf16[1,16,2048]{2,0,1:T(2,128)(2,1)} %get-tuple-element.9, s32[16]{0:T(128)S(1)} %bitcast.116, ...), kind=kOutput, calls=%fused_computation.20 | convolution fusion | flops 5242944 | bytes 1310800 | tf_op jit(solution)/shard_map/nh,hrc->nrc/dot_general | solution.py:78
  103.3 0.7 fusion.10
  104.0 11.1 %psum.75 = f32[18,16]{1,0:T(8,128)S(1)} all-reduce(f32[18,16]{1,0:T(8,128)S(1)} %pad_maximum_fusion.2), channel_id=1, replica_groups=mesh['groups'=2,'replica'=4,'tensor'=4] {'tensor'}, use_global_device_ids=true, to_apply=%region_13.15 | all-reduce | flops 288 | bytes 2304 | tf_op jit(solution)/shard_map/psum | solution.py:115
  115.1 0.2 fusion.31
  115.3 0.0 copy-done.2
  115.3 0.0 copy-done.3
  115.3 0.0 copy-done.4
  115.4 0.0 copy-done.5
  115.4 0.9 fusion.20
  116.3 1.2 fusion.8
  117.6 0.7 pad_maximum_fusion
  (24 shorter events, 0.2 us)
Async XLA Ops:
  10.1 42.4 %all-to-all-start = ((s32[4,1,1]{2,1,0:T(1,128)}), s32[4,1,1]{2,1,0:T(1,128)S(1)}, u32[]{:S(2)}, u32[]{:S(2)}) async-start(s32[4,1,1]{2,1,0:T(1,128)} %copy.78), calls=%async_computation | async-start | bytes 4096 | tf_op jit(solution)/shard_map/all_to_all | solution.py:98
  16.5 84.6 %all-reduce.3.cloned.1.call-start = ((), (), s32[]{:S(2)}) async-start(), calls=%async_computation.3 | async-start | bytes 2097152 | tf_op jit(solution)/shard_map/psum | solution.py:14
  43.5 2.7 %copy-start = (bf16[18,2048]{1,0:T(8,128)(2,1)S(1)}, bf16[18,2048]{1,0:T(8,128)(2,1)}, u32[]{:S(2)}) copy-start(bf16[18,2048]{1,0:T(8,128)(2,1)} %param.9) | copy-start | bytes 221188
  43.5 2.8 %copy-start.1 = (s32[18]{0:T(128)S(1)}, s32[18]{0:T(128)}, u32[]{:S(2)}) copy-start(s32[18]{0:T(128)} %param.11) | copy-start | bytes 220
  52.4 48.7 %copy-start.6 = (s32[18]{0:T(128)S(1)}, s32[18]{0:T(128)}, u32[]{:S(2)}) copy-start(s32[18]{0:T(128)} %param.13) | copy-start | bytes 220
  53.9 19.0 %all-to-all-start.1 = ((bf16[4,1,16,2048]{3,2,1,0:T(8,128)(2,1)}), bf16[4,1,16,2048]{3,2,1,0:T(8,128)(2,1)S(1)}, u32[]{:S(2)}, u32[]{:S(2)}) async-start(bf16[4,1,16,2048]{3,2,1,0:T(8,128)(2,1)} %copy.80), calls=%async_computation.1 | async-start | bytes 524288 | tf_op jit(solution)/shard_map/all_to_all | solution.py:105
  72.9 10.2 %all-to-all-start.2 = ((bf16[4,1,16,2048]{3,2,1,0:T(8,128)(2,1)}), bf16[4,1,16,2048]{3,2,1,0:T(8,128)(2,1)S(1)}, u32[]{:S(2)}, u32[]{:S(2)}) async-start(bf16[4,1,16,2048]{3,2,1,0:T(8,128)(2,1)} %copy.86), calls=%async_computation.2 | async-start | bytes 524288 | tf_op jit(solution)/shard_map/all_to_all | solution.py:106
  101.1 14.2 %copy-start.2 = (bf16[1,16,2048]{2,0,1:T(2,128)(2,1)S(1)}, bf16[1,16,2048]{2,0,1:T(2,128)(2,1)}, u32[]{:S(2)}) copy-start(bf16[1,16,2048]{2,0,1:T(2,128)(2,1)} %get-tuple-element.10) | copy-start | bytes 196612
  101.1 14.2 %copy-start.3 = (bf16[1,16,2048]{2,0,1:T(2,128)(2,1)S(1)}, bf16[1,16,2048]{2,0,1:T(2,128)(2,1)}, u32[]{:S(2)}) copy-start(bf16[1,16,2048]{2,0,1:T(2,128)(2,1)} %get-tuple-element.11) | copy-start | bytes 196612
  101.1 14.2 %copy-start.4 = (bf16[1,16,2048]{2,0,1:T(2,128)(2,1)S(1)}, bf16[1,16,2048]{2,0,1:T(2,128)(2,1)}, u32[]{:S(2)}) copy-start(bf16[1,16,2048]{2,0,1:T(2,128)(2,1)} %get-tuple-element.12) | copy-start | bytes 196612
  101.1 14.2 %copy-start.5 = (bf16[1,16,2048]{2,0,1:T(2,128)(2,1)S(1)}, bf16[1,16,2048]{2,0,1:T(2,128)(2,1)}, u32[]{:S(2)}) copy-start(bf16[1,16,2048]{2,0,1:T(2,128)(2,1)} %get-tuple-element.13) | copy-start | bytes 196612
Sparse Core Ops, SparseCore 0:
  43.6 57.4 all-reduce.2
where the time goes:
time: 126 us; the launch traced here: 125 us
  waiting for transfers between devices  37.8 us (30%)
  between operations  25.2 us (20%)
  blocking collectives  19.9 us (16%)
  starting transfers between devices  13.2 us (10%)
  local copies, waits for them, and re-layouts  12.9 us (10%)
  matrix products  8.78 us (7%)
  other arithmetic  7.4 us (6%)
    psum x1, waiting for transfers between devices, broadcast(): return lax.psum(block, axis)  17.2 us
    all_to_all x1, waiting for transfers between devices, on_device(): lax.all_to_all(send_down, 'replica', split_axis=0, concat_axis=0, tiled=T...  14.4 us
    psum x1, blocking collectives, on_device(): lax.psum(jnp.concatenate([stay_partial, moved_partial], axis=0), 'tensor')  11.1 us
    psum x1, blocking collectives, on_device(): usage = lax.psum(usage, 'replica')  8.8 us
    all_to_all x1, starting transfers between devices, on_device(): lax.all_to_all(wanted[:, None], 'replica', split_axis=0, concat_axis=0, t...  6.35 us
    all_to_all x1, waiting for transfers between devices, on_device(): lax.all_to_all(send_up, 'replica', split_axis=0, concat_axis=0, tiled=True)  6.15 us
    unnamed x24, local copies, waits for them, and re-layouts  4.62 us
    all_to_all x1, starting transfers between devices, on_device(): lax.all_to_all(send_up, 'replica', split_axis=0, concat_axis=0, tiled=True)  3.4 us
  transfers between devices with their start and end apart: 4, of which 3 were waited for; matrix products, arithmetic and copies ran while one was open for 16% of the time, Pallas kernels for 0%

commit v1 on v0

--- a/solution.py
+++ b/solution.py
@@ -54,7 +54,9 @@
     stay_index = adapter_index[:STAY]
     catalog = jnp.arange(total_adapters, dtype=jnp.int32)
     usage = jnp.sum((stay_index[:, None] == catalog[None, :]).astype(jnp.int32), axis=0)
-    usage = lax.psum(usage, "replica")
+    usage = usage
+    for hop in (1, 2):
+        usage = usage + lax.ppermute(usage, "replica", [(dev, dev ^ hop) for dev in range(4)])
     ranking = jnp.where(usage > 0, total_adapters - catalog, 0)
     hot_index = total_adapters - lax.top_k(ranking, hot_total)[0]
     down_list = []

time: 126 us -> 137 us (1.087)
  waiting for transfers between devices: 37.8 us -> 52.8 us
  blocking collectives: 19.9 us -> 11.1 us
  starting transfers between devices: 13.2 us -> 18.3 us
  other arithmetic: 7.4 us -> 9.72 us
    psum x1, waiting for transfers between devices: 17.2 us -> 36.3 us  [broadcast(): return lax.psum(block, axis)]
    all_to_all x1, waiting for transfers between devices: 14.4 us -> 0.01 us  [on_device(): lax.all_to_all(send_down, 'replica', split_axis=0, concat_axis=0, tiled=T...]
    psum x1 -> x0, blocking collectives: 8.8 us -> none  [on_device(): usage = lax.psum(usage, 'replica')]
    all_to_all x1, waiting for transfers between devices: 6.15 us -> 13.1 us  [on_device(): lax.all_to_all(send_up, 'replica', split_axis=0, concat_axis=0, tiled=True)]
    ppermute x0 -> x2, starting transfers between devices: none -> 4.95 us  [on_device(): lax.ppermute(usage, 'replica', [(dev, dev ^ hop) for dev in range(4)])]
    ppermute x0 -> x2, waiting for transfers between devices: none -> 3.47 us  [on_device(): lax.ppermute(usage, 'replica', [(dev, dev ^ hop) for dev in range(4)])]
    unnamed x24 -> x32, local copies, waits for them, and re-layouts: 4.62 us -> 3.01 us
  transfers between devices with their start and end apart: 4 -> 6, of which waited for: 3 -> 3; matrix products, arithmetic and copies ran while one was open for 16% -> 14% of each run, Pallas kernels for 0% -> 0%
where the time goes in v1:
time: 137 us
  waiting for transfers between devices  52.8 us (39%)
  between operations  25.3 us (18%)
  starting transfers between devices  18.3 us (13%)
  local copies, waits for them, and re-layouts  11.8 us (9%)
  blocking collectives  11.1 us (8%)
  other arithmetic  9.72 us (7%)
  matrix products  7.55 us (6%)
    psum x1, waiting for transfers between devices, broadcast(): return lax.psum(block, axis)  36.3 us
    all_to_all x1, waiting for transfers between devices, on_device(): lax.all_to_all(send_up, 'replica', split_axis=0, concat_axis=0, tiled=True)  13.1 us
    psum x1, blocking collectives, on_device(): lax.psum(jnp.concatenate([stay_partial, moved_partial], axis=0), 'tensor')  11.1 us
    all_to_all x1, starting transfers between devices, on_device(): lax.all_to_all(wanted[:, None], 'replica', split_axis=0, concat_axis=0, t...  6.35 us
    ppermute x2, starting transfers between devices, on_device(): lax.ppermute(usage, 'replica', [(dev, dev ^ hop) for dev in range(4)])  4.95 us
    all_to_all x1, starting transfers between devices, on_device(): lax.all_to_all(send_down, 'replica', split_axis=0, concat_axis=0, tiled=T...  3.63 us
    ppermute x2, waiting for transfers between devices, on_device(): lax.ppermute(usage, 'replica', [(dev, dev ^ hop) for dev in range(4)])  3.47 us
    all_to_all x1, starting transfers between devices, on_device(): lax.all_to_all(send_up, 'replica', split_axis=0, concat_axis=0, tiled=True)  3.42 us
  transfers between devices with their start and end apart: 6, of which 3 were waited for; matrix products, arithmetic and copies ran while one was open for 14% of the time, Pallas kernels for 0%

profile of v1, /device:TPU:0, one launch (start us, length us, event | category | flops | bytes accessed | tf_op | source)
XLA Modules:
  0.0 136.7 jit_solution(10653504597398017137)
XLA Ops:
  7.2 1.3 compare_and_fusion
  8.4 0.7 slice.70
  9.1 0.1 fusion.54
  9.2 0.1 select_reduce_fusion
  9.3 0.6 gather_fusion
  10.0 0.7 copy.78
  10.7 6.3 %all-to-all-start = ((s32[4,1,1]{2,1,0:T(1,128)}), s32[4,1,1]{2,1,0:T(1,128)S(1)}, u32[]{:S(2)}, u32[]{:S(2)}) async-start(s32[4,1,1]{2,1,0:T(1,128)} %copy.78), calls=%async_computation | async-start | bytes 4096 | tf_op jit(solution)/shard_map/all_to_all | solution.py:100
  17.0 1.3 convert_reduce_fusion
  18.3 2.0 %collective-permute-start = (s32[16]{0:T(128)}, s32[16]{0:T(128)}, u32[]{:S(2)}, u32[]{:S(2)}) collective-permute-start(s32[16]{0:T(128)} %convert_reduce_fusion), channel_id=1, source_target_pairs={{0,4},{4,0},{8,12},{12,8},{1,5},{5,1},{9,13},{13,9},{2,6},{6,2},{1... | collective-permute-start | bytes 200 | tf_op jit(solution)/shard_map/ppermute | solution.py:59
  20.3 1.0 fusion.66
  21.3 1.7 %fusion.65 = (bf16[1,16,128,256]{3,2,1,0:T(8,128)(2,1)S(1)}, bf16[1,16,128,256]{3,2,1,0:T(8,128)(2,1)S(1)}) fusion(bf16[2,18,128,256]{3,2,1,0:T(8,128)(2,1)} %param.10), kind=kLoop, calls=%fused_computation.114 | loop fusion | bytes 4194304 | tf_op jit(solution)/shard_map/slice | solution.py:83
  23.0 0.0 copy-done.1
  23.1 0.0 copy-done.3
  23.1 0.1 iota_compare_fusion
  23.1 0.6 compare_select_fusion
  23.7 0.1 copy.105
  23.9 0.1 copy.104
  24.0 0.1 fusion.7
  24.1 0.2 fusion.68
  24.3 0.2 convolution_convert_fusion
  24.5 0.6 reshape.223
  25.2 0.7 copy.103
  25.9 0.7 copy.102
  26.6 0.4 fusion.4
  26.9 0.2 fusion.69
  27.8 0.0 copy-done
  27.8 0.2 copy.73
  28.1 0.0 copy-done.4
  28.1 1.2 copy.81
  29.2 0.7 fusion.37
  29.9 0.1 fusion.28
  30.0 0.0 all-to-all-done
  30.0 0.2 reduce
  30.2 0.4 convolution_bitcast_fusion.1
  30.6 0.8 copy.80
  31.4 3.6 %all-to-all-start.1 = ((bf16[4,1,16,2048]{3,2,1,0:T(8,128)(2,1)}), bf16[4,1,16,2048]{3,2,1,0:T(8,128)(2,1)S(1)}, u32[]{:S(2)}, u32[]{:S(2)}) async-start(bf16[4,1,16,2048]{3,2,1,0:T(8,128)(2,1)} %copy.80), calls=%async_computation.1 | async-start | bytes 524288 | tf_op jit(solution)/shard_map/all_to_all | solution.py:107
  35.0 0.0 all-reduce.3.cloned.1.call-start
  35.0 0.3 convolution_bitcast_fusion
  35.4 0.0 collective-permute-done
  35.4 0.7 add.99
  36.1 2.9 %collective-permute-start.1 = (s32[16]{0:T(128)S(1)}, s32[16]{0:T(128)S(1)}, u32[]{:S(2)}, u32[]{:S(2)}) collective-permute-start(s32[16]{0:T(128)S(1)} %add.99), channel_id=1, source_target_pairs={{0,8},{4,12},{8,0},{12,4},{1,9},{5,13},{9,1},{13,5},{2,10},{6,14},... | collective-permute-start | bytes 200 | tf_op jit(solution)/shard_map/ppermute | solution.py:59
  39.0 0.8 copy.86
  39.9 3.5 %collective-permute-done.1 = s32[16]{0:T(128)S(1)} collective-permute-done((s32[16]{0:T(128)S(1)}, s32[16]{0:T(128)S(1)}, u32[]{:S(2)}, u32[]{:S(2)}) %collective-permute-start.1) | collective-permute-done | bytes 96 | tf_op jit(solution)/shard_map/ppermute | solution.py:59
  43.3 1.2 top_k.9
  44.6 0.7 fusion.67
  54.8 0.0 copy-start.9
  55.6 1.4 %broadcast_select_fusion.7 = (bf16[1,16,2048]{2,0,1:T(2,128)(2,1)}, bf16[1,16,2048]{2,0,1:T(2,128)(2,1)}, bf16[1,16,2048]{2,0,1:T(2,128)(2,1)}, bf16[1,16,2048]{2,0,1:T(2,128)(2,1)}) fusion(pred[]{:T(512)S(6)} %eq.87, bf16[4,16,2048]{2,0,1:T(4,128)(2,1)S(1)} %copy.73, s32[]{:T(128)S(6)} %select_n.215, s32[]{:T(128)S(6)} %select_n.233, pred[]{:T(512)S(6)} %eq.90, ...), kind=kLoop, calls=%fused_computation.43 | loop fusion | flops 131072 | bytes 524308 | tf_op jit(solution)/shard_map/jit(_where)/select_n | solution.py:13
  57.0 1.4 %broadcast_select_fusion.6 = (bf16[1,16,2048]{2,0,1:T(2,128)(2,1)}, bf16[1,16,2048]{2,0,1:T(2,128)(2,1)}, bf16[1,16,2048]{2,0,1:T(2,128)(2,1)}, bf16[1,16,2048]{2,0,1:T(2,128)(2,1)}) fusion(pred[]{:T(512)S(6)} %eq.87, bf16[4,16,2048]{2,0,1:T(4,128)(2,1)S(1)} %copy.81, s32[]{:T(128)S(6)} %select_n.215, s32[]{:T(128)S(6)} %select_n.233, pred[]{:T(512)S(6)} %eq.90, ...), kind=kLoop, calls=%fused_computation.42 | loop fusion | flops 131072 | bytes 524308 | tf_op jit(solution)/shard_map/jit(_where)/select_n | solution.py:13
  58.4 0.0 all-reduce.3.cloned.1.call-update
  58.5 0.0 all-to-all-done.1
  58.5 3.4 %all-to-all-start.2 = ((bf16[4,1,16,2048]{3,2,1,0:T(8,128)(2,1)}), bf16[4,1,16,2048]{3,2,1,0:T(8,128)(2,1)S(1)}, u32[]{:S(2)}, u32[]{:S(2)}) async-start(bf16[4,1,16,2048]{3,2,1,0:T(8,128)(2,1)} %copy.86), calls=%async_computation.2 | async-start | bytes 524288 | tf_op jit(solution)/shard_map/all_to_all | solution.py:108
  61.9 0.1 fusion.84
  62.0 0.6 gather_fusion.1
  62.5 13.1 %all-to-all-done.2 = bf16[4,1,16,2048]{3,2,1,0:T(8,128)(2,1)S(1)} async-done(((bf16[4,1,16,2048]{3,2,1,0:T(8,128)(2,1)}), bf16[4,1,16,2048]{3,2,1,0:T(8,128)(2,1)S(1)}, u32[]{:S(2)}, u32[]{:S(2)}) %all-to-all-start.2) | async-done | bytes 262176 | tf_op jit(solution)/shard_map/all_to_all | solution.py:108
  75.6 0.6 gather_fusion.2
  76.2 0.2 fusion.33
  76.4 36.3 %all-reduce.3.cloned.1.call-done = (bf16[1,16,2048]{2,0,1:T(2,128)(2,1)}, bf16[1,16,2048]{2,0,1:T(2,128)(2,1)}, bf16[1,16,2048]{2,0,1:T(2,128)(2,1)}, bf16[1,16,...) async-done(((bf16[1,16,2048]{2,0,1:T(2,128)(2,1)}, ...) | async-done | bytes 524304 | tf_op jit(solution)/shard_map/psum | solution.py:14
  112.7 2.1 %fusion.12 = bf16[16,16,2048]{2,0,1:T(8,128)(2,1)S(1)} fusion(bf16[1,16,2048]{2,0,1:T(2,128)(2,1)} %get-tuple-element.6, bf16[1,16,2048]{2,0,1:T(2,128)(2,1)} %get-tuple-element.7, bf16[1,16,2048]{2,0,1:T(2,128)(2,1)} %get-tuple-element.8, bf16[1,16,2048]{2,0,1:T(2,128)(2,1)} %get-tuple-element.9, s32[16]{0:T(128)S(1)} %bitcast.116, ...), kind=kOutput, calls=%fused_computation.20 | convolution fusion | flops 5242944 | bytes 1310800 | tf_op jit(solution)/shard_map/nh,hrc->nrc/dot_general | solution.py:80
  114.8 0.7 fusion.10
  115.5 11.1 %psum.67 = f32[18,16]{1,0:T(8,128)S(1)} all-reduce(f32[18,16]{1,0:T(8,128)S(1)} %pad_maximum_fusion.2), channel_id=1, replica_groups=mesh['groups'=2,'replica'=4,'tensor'=4] {'tensor'}, use_global_device_ids=true, to_apply=%region_12.14 | all-reduce | flops 288 | bytes 2304 | tf_op jit(solution)/shard_map/psum | solution.py:117
  126.6 0.2 fusion.31
  126.9 0.9 fusion.20
  127.8 1.2 fusion.8
  129.1 0.7 pad_maximum_fusion
  (36 shorter events, 0.2 us)
Async XLA Ops:
  10.7 19.4 %all-to-all-start = ((s32[4,1,1]{2,1,0:T(1,128)}), s32[4,1,1]{2,1,0:T(1,128)S(1)}, u32[]{:S(2)}, u32[]{:S(2)}) async-start(s32[4,1,1]{2,1,0:T(1,128)} %copy.78), calls=%async_computation | async-start | bytes 4096 | tf_op jit(solution)/shard_map/all_to_all | solution.py:100
  18.3 4.7 %copy-start.1 = (bf16[18,2048]{1,0:T(8,128)(2,1)S(1)}, bf16[18,2048]{1,0:T(8,128)(2,1)}, u32[]{:S(2)}) copy-start(bf16[18,2048]{1,0:T(8,128)(2,1)} %param.9) | copy-start | bytes 221188
  18.3 4.7 %copy-start.3 = (s32[18]{0:T(128)S(1)}, s32[18]{0:T(128)}, u32[]{:S(2)}) copy-start(s32[18]{0:T(128)} %param.11) | copy-start | bytes 220
  18.3 17.1 %collective-permute-start = (s32[16]{0:T(128)}, s32[16]{0:T(128)}, u32[]{:S(2)}, u32[]{:S(2)}) collective-permute-start(s32[16]{0:T(128)} %convert_reduce_fusion), channel_id=1, source_target_pairs={{0,4},{4,0},{8,12},{12,8},{1,5},{5,1},{9,13},{13,9},{2,6},{6,2},{1... | collective-permute-start | bytes 200 | tf_op jit(solution)/shard_map/ppermute | solution.py:59
  25.2 2.6 %copy-start = (bf16[4,16,2048]{2,1,0:T(8,128)(2,1)S(1)}, bf16[4,16,2048]{2,1,0:T(8,128)(2,1)}, u32[]{:S(2)}) copy-start(bf16[4,16,2048]{2,1,0:T(8,128)(2,1)} %param.14) | copy-start | bytes 786436
  25.9 2.2 %copy-start.4 = (s32[2]{0:T(128)S(1)}, s32[2]{0:T(128)}, u32[]{:S(2)}) copy-start(s32[2]{0:T(128)} %compare_select_fusion) | copy-start | bytes 28
  31.4 27.0 %all-to-all-start.1 = ((bf16[4,1,16,2048]{3,2,1,0:T(8,128)(2,1)}), bf16[4,1,16,2048]{3,2,1,0:T(8,128)(2,1)S(1)}, u32[]{:S(2)}, u32[]{:S(2)}) async-start(bf16[4,1,16,2048]{3,2,1,0:T(8,128)(2,1)} %copy.80), calls=%async_computation.1 | async-start | bytes 524288 | tf_op jit(solution)/shard_map/all_to_all | solution.py:107
  35.0 77.6 %all-reduce.3.cloned.1.call-start = ((), (), s32[]{:S(2)}) async-start(), calls=%async_computation.3 | async-start | bytes 2097152 | tf_op jit(solution)/shard_map/psum | solution.py:14
  36.1 7.2 %collective-permute-start.1 = (s32[16]{0:T(128)S(1)}, s32[16]{0:T(128)S(1)}, u32[]{:S(2)}, u32[]{:S(2)}) collective-permute-start(s32[16]{0:T(128)S(1)} %add.99), channel_id=1, source_target_pairs={{0,8},{4,12},{8,0},{12,4},{1,9},{5,13},{9,1},{13,5},{2,10},{6,14},... | collective-permute-start | bytes 200 | tf_op jit(solution)/shard_map/ppermute | solution.py:59
  39.9 36.3 %copy-start.2 = (bf16[2,2048,1]{1,2,0:T(2,128)(2,1)S(1)}, bf16[2,2048,1]{1,2,0:T(2,128)(2,1)}, u32[]{:S(2)}) copy-start(bf16[2,2048,1]{1,2,0:T(2,128)(2,1)} %reshape.223) | copy-start | bytes 24580
  39.9 36.3 %copy-start.10 = (pred[2]{0:T(512)(128)(4,1)S(1)}, pred[2]{0:T(512)(128)(4,1)}, u32[]{:S(2)}) copy-start(pred[2]{0:T(512)(128)(4,1)} %get-tuple-element.14) | copy-start | bytes 10
  54.8 57.9 %copy-start.9 = (s32[18]{0:T(128)S(1)}, s32[18]{0:T(128)}, u32[]{:S(2)}) copy-start(s32[18]{0:T(128)} %param.13) | copy-start | bytes 220
  58.5 17.2 %all-to-all-start.2 = ((bf16[4,1,16,2048]{3,2,1,0:T(8,128)(2,1)}), bf16[4,1,16,2048]{3,2,1,0:T(8,128)(2,1)S(1)}, u32[]{:S(2)}, u32[]{:S(2)}) async-start(bf16[4,1,16,2048]{3,2,1,0:T(8,128)(2,1)} %copy.86), calls=%async_computation.2 | async-start | bytes 524288 | tf_op jit(solution)/shard_map/all_to_all | solution.py:108
  112.7 14.2 %copy-start.5 = (bf16[1,16,2048]{2,0,1:T(2,128)(2,1)S(1)}, bf16[1,16,2048]{2,0,1:T(2,128)(2,1)}, u32[]{:S(2)}) copy-start(bf16[1,16,2048]{2,0,1:T(2,128)(2,1)} %get-tuple-element.10) | copy-start | bytes 196612
  112.7 14.2 %copy-start.6 = (bf16[1,16,2048]{2,0,1:T(2,128)(2,1)S(1)}, bf16[1,16,2048]{2,0,1:T(2,128)(2,1)}, u32[]{:S(2)}) copy-start(bf16[1,16,2048]{2,0,1:T(2,128)(2,1)} %get-tuple-element.11) | copy-start | bytes 196612
  112.7 14.2 %copy-start.7 = (bf16[1,16,2048]{2,0,1:T(2,128)(2,1)S(1)}, bf16[1,16,2048]{2,0,1:T(2,128)(2,1)}, u32[]{:S(2)}) copy-start(bf16[1,16,2048]{2,0,1:T(2,128)(2,1)} %get-tuple-element.12) | copy-start | bytes 196612
  112.7 14.2 %copy-start.8 = (bf16[1,16,2048]{2,0,1:T(2,128)(2,1)S(1)}, bf16[1,16,2048]{2,0,1:T(2,128)(2,1)}, u32[]{:S(2)}) copy-start(bf16[1,16,2048]{2,0,1:T(2,128)(2,1)} %get-tuple-element.13) | copy-start | bytes 196612
Sparse Core Ops, SparseCore 0:
  58.6 54.0 all-reduce.2
